TPU v7x, 32 devices: a whole 2x2x4 slice. The times are simulated.
32 devices in a mesh: item: 8 (over y, x, core), dp: 4 (over z).
Axes of the slice: x: 2, y: 2, z: 4, core: 2. Of those that a mesh axis runs over, the one named last changes fastest.
Arguments:
- hidden_states: bfloat16 [32768, 512], P(('item', 'dp'))
- item_table: bfloat16 [4096, 512], P('item'), may hold values from -0.25 to 0.25
- cand_local: int32 [64], replicated, may hold values from 0 to 511
- log_sample: float32 [64], replicated, may hold values from -14 to -4
- target_slot: int32 [32768], P(('item', 'dp')), may hold values from 0 to 63
- loss_weight: float32 [32768], P(('item', 'dp')), may hold values from -6 to 6
Outputs:
- grad_hidden: bfloat16 [32768, 512], P(('item', 'dp'))
- grad_table: float32 [4096, 512], P('item')
Inputs may be any that keep to these rules, and one draw needn't show every extreme that they name: Candidate slot s belongs to the item shard s // 8; cand_local counts rows within that shard, and a row may be sampled more than once.
All inputs are finite; a program needn't handle non-finite values.
Results may differ from a plain program's by a relative error of at most 0.0049.
Values may be sent and summed in bfloat16 or wider, within the bound.
No kernel may reach another device: no remote copies, remote signals or barrier semaphores. Data moves between devices by JAX's collectives and lax.ppermute only.
A program may use at most 64 MiB of HBM per device.

v0:
```python
import math
import jax
import jax.numpy as jnp
from jax import lax
from jax.sharding import PartitionSpec as P


def on_device(hidden_states, item_table, cand_local, log_sample, target_slot, loss_weight):
    owners = lax.axis_size("item")
    total_cands = log_sample.shape[0]
    per_owner = total_cands // owners
    my_index = lax.axis_index("item")
    my_local = lax.dynamic_slice_in_dim(cand_local, my_index * per_owner, per_owner)
    my_rows = item_table[my_local]
    cand_rows = lax.all_gather(my_rows, "item", axis=0, tiled=True)
    slots = jnp.arange(total_cands, dtype=jnp.int32)
    tok_rows = hidden_states.shape[0]
    width = hidden_states.shape[1]
    block = math.gcd(tok_rows, 512)
    count = tok_rows // block
    states = hidden_states.reshape(count, block, width)
    targets = target_slot.reshape(count, block)
    weights = loss_weight.reshape(count, block)

    def step(total, inputs):
        rows, tgt, wts = inputs
        logits = (
            jnp.dot(rows, cand_rows.T, preferred_element_type=jnp.float32) - log_sample[None, :]
        )
        probs = jax.nn.softmax(logits, axis=1)
        onehot = (tgt[:, None] == slots[None, :]).astype(jnp.float32)
        grad_logits = (wts[:, None] * (probs - onehot)).astype(jnp.bfloat16)
        grad_rows = jnp.dot(grad_logits, cand_rows, preferred_element_type=jnp.float32).astype(
            jnp.bfloat16
        )
        total = total + jnp.dot(grad_logits.T, rows, preferred_element_type=jnp.float32)
        return (total, grad_rows)

    partial_grad, grad_blocks = lax.scan(
        step, jnp.zeros((total_cands, width), jnp.float32), (states, targets, weights)
    )
    grad_hidden = grad_blocks.reshape(tok_rows, width)
    owned = lax.psum_scatter(partial_grad, "item", scatter_dimension=0, tiled=True)
    owned = lax.psum(owned, "dp")
    table_rows = item_table.shape[0]
    placing = (my_local[:, None] == jnp.arange(table_rows, dtype=jnp.int32)[None, :]).astype(
        jnp.float32
    )
    grad_table = jnp.dot(
        placing.T, owned, preferred_element_type=jnp.float32, precision=lax.Precision.HIGHEST
    )
    return (grad_hidden, grad_table)


def solution(mesh):
    placed = (
        P(("item", "dp"), None),
        P("item", None),
        P(),
        P(),
        P(("item", "dp")),
        P(("item", "dp")),
    )
    return jax.shard_map(
        on_device,
        mesh=mesh,
        in_specs=placed,
        out_specs=(P(("item", "dp"), None), P("item", None)),
        check_vma=False,
    )
```

profile of v0, /device:TPU:0, one launch (start us, length us, event | category | flops | bytes accessed | tf_op | source)
XLA Modules:
  0.0 87.7 jit_solution(3988291975070287816)
XLA Ops:
  7.2 0.0 copy-start
  7.2 0.0 reduce-scatter.2.cloned.1.call-start
  7.3 0.0 copy-start.6
  7.3 0.7 copy-done.6
  8.0 0.1 compare_select_fusion
  8.0 0.2 copy-done
  8.2 0.6 gather_fusion
  8.8 0.0 copy-start.4
  8.8 10.7 %all-gather = bf16[64,512]{1,0:T(8,128)(2,1)S(1)} all-gather(bf16[8,512]{1,0:T(8,128)(2,1)S(1)} %gather_fusion), channel_id=2, replica_groups=mesh['item'=8,'dp'=4] {'item'}, dimensions={0}, use_global_device_ids=true | all-gather | bytes 73728 | tf_op jit(solution)/shard_map/all_gather | solution.py:15
  19.5 0.0 copy-done.4
  19.6 0.7 copy-done.5
  20.2 0.0 copy-start.3
  20.2 0.7 copy-done.3
  20.9 4.2 %while.13 = (s32[]{:T(128)}, f32[64,512]{1,0:T(8,128)S(1)}, bf16[2,512,512]{2,1,0:T(8,128)(2,1)S(1)}, f32[2,512]{1,0:T(2,128)S(1)}, bf16[2,512,512]{2,1,0:T(8,12...) while((s32[]{:T(128)}, f32[64,512]{1,0:T(8,128)S(1)}, ...), condition=%wide.region_3.4_spmd.clone, body=%wide.region_0.3_spmd.clone.sunk | while | flops 101579776 | bytes 6716315 | solution.py:39
  20.9 0.0 copy-start.1
  20.9 1.4 %fusion.26 = (f32[512]{0:T(512)S(1)}, f32[512,64]{0,1:T(8,128)S(1)}) fusion(f32[64]{0:T(128)S(1)} %get-tuple-element.180, bf16[64,512]{1,0:T(8,128)(2,1)S(1)} %get-tuple-element.179, bf16[2,512,512]{2,1,0:T(8,128)(2,1)} %get-tuple-element.178, s32[]{:T(128)} %get-tuple-element.164), kind=kOutput, calls=%fused_computation.24.clone.1 | convolution fusion | flops 33619456 | bytes 723712 | tf_op jit(solution)/shard_map/while/body/eval_jaxpr/dot_general | solution.py:28
  22.4 0.3 fusion.28
  22.8 0.0 copy-done.1
  22.8 0.2 convolution_add_fusion.2
  23.0 0.0 copy-start.1
  23.0 1.4 %fusion.26 = (f32[512]{0:T(512)S(1)}, f32[512,64]{0,1:T(8,128)S(1)}) fusion(f32[64]{0:T(128)S(1)} %get-tuple-element.180, bf16[64,512]{1,0:T(8,128)(2,1)S(1)} %get-tuple-element.179, bf16[2,512,512]{2,1,0:T(8,128)(2,1)} %get-tuple-element.178, s32[]{:T(128)} %get-tuple-element.164), kind=kOutput, calls=%fused_computation.24.clone.1 | convolution fusion | flops 33619456 | bytes 723712 | tf_op jit(solution)/shard_map/while/body/eval_jaxpr/dot_general | solution.py:28
  24.5 0.3 fusion.28
  24.9 0.0 copy-done.1
  24.9 0.2 convolution_add_fusion.2
  25.1 0.0 copy-start.2
  25.2 0.0 copy-start.7
  25.2 0.6 copy-done.2
  25.8 0.0 reduce-scatter.2.cloned.1.call-update
  25.8 34.0 %reduce-scatter.2.cloned.1.call-done = f32[8,512]{1,0:T(8,128)} async-done(((f32[64,512]{1,0:T(8,128)}), f32[8,512]{1,0:T(8,128)}) %reduce-scatter.2.cloned.1.call-update) | async-done | bytes 16400 | tf_op jit(solution)/shard_map/reduce_scatter | solution.py:43
  59.8 19.4 %psum.7 = f32[8,512]{1,0:T(8,128)S(1)} all-reduce(f32[8,512]{1,0:T(8,128)} %reduce-scatter.2.cloned.1.call-done), channel_id=1, replica_groups=mesh['item'=8,'dp'=4] {'dp'}, use_global_device_ids=true, to_apply=%region_5.6 | all-reduce | flops 4096 | bytes 32768 | tf_op jit(solution)/shard_map/psum | solution.py:44
  79.2 1.7 %fusion.11 = f32[512,512]{1,0:T(8,128)} fusion(f32[8,512]{1,0:T(8,128)S(1)} %psum.7, s32[8]{0:T(128)S(1)} %get-tuple-element.98), kind=kOutput, calls=%fused_computation.20 | convolution fusion | flops 25169920 | bytes 1064992 | tf_op jit(solution)/shard_map/dot_general | solution.py:49
  80.8 0.0 copy-done.7
  (12 shorter events, 0.2 us)
Async XLA Ops:
  7.2 1.1 %copy-start = (bf16[512,512]{1,0:T(8,128)(2,1)S(1)}, bf16[512,512]{1,0:T(8,128)(2,1)}, u32[]{:S(2)}) copy-start(bf16[512,512]{1,0:T(8,128)(2,1)} %param.9) | copy-start | bytes 1572868
  7.2 52.6 %reduce-scatter.2.cloned.1.call-start = ((), (), s32[]{:S(2)}) async-start(), calls=%async_computation.1 | async-start | bytes 147456 | tf_op jit(solution)/shard_map/reduce_scatter | solution.py:43
  7.3 0.7 copy-start.6
  8.8 10.7 %copy-start.4 = (f32[1024]{0:T(1024)S(1)}, f32[1024]{0:T(1024)}, u32[]{:S(2)}) copy-start(f32[1024]{0:T(1024)} %param.13) | copy-start | bytes 12292
  19.5 0.7 copy-start.5
  20.2 0.7 copy-start.3
  20.9 1.9 %copy-start.1 = (bf16[2,512,512]{2,1,0:T(8,128)(2,1)S(1)}, bf16[2,512,512]{2,1,0:T(8,128)(2,1)}, u32[]{:S(2)}) copy-start(bf16[2,512,512]{2,1,0:T(8,128)(2,1)} %get-tuple-element.178) | copy-start | bytes 3145732 | tf_op jit(solution)/shard_map/while
  23.0 1.9 %copy-start.1 = (bf16[2,512,512]{2,1,0:T(8,128)(2,1)S(1)}, bf16[2,512,512]{2,1,0:T(8,128)(2,1)}, u32[]{:S(2)}) copy-start(bf16[2,512,512]{2,1,0:T(8,128)(2,1)} %get-tuple-element.178) | copy-start | bytes 3145732 | tf_op jit(solution)/shard_map/while
  25.1 0.7 copy-start.2
  25.2 55.7 %copy-start.7 = (bf16[2,512,512]{2,1,0:T(8,128)(2,1)}, bf16[2,512,512]{2,1,0:T(8,128)(2,1)S(1)}, u32[]{:S(2)}) copy-start(bf16[2,512,512]{2,1,0:T(8,128)(2,1)S(1)} %get-tuple-element.50) | copy-start | bytes 3145732
Sparse Core Ops, SparseCore 0:
  26.0 33.8 reduce-scatter.1
where the time goes:
time: 88 us; the launch traced here: 87.7 us
  waiting for transfers between devices  34 us (39%)
  blocking collectives  30.1 us (34%)
  between operations  14.1 us (16%)
  matrix products  5.64 us (6%)
  local copies, waits for them, and re-layouts  3.5 us (4%)
    reduce_scatter x1, waiting for transfers between devices, on_device(): lax.psum_scatter(partial_grad, 'item', scatter_dimension=0, tiled=True)  34 us
    psum x1, blocking collectives, on_device(): owned = lax.psum(owned, 'dp')  19.4 us
    all_gather x1, blocking collectives, on_device(): cand_rows = lax.all_gather(my_rows, 'item', axis=0, tiled=True)  10.7 us
    unnamed x14, local copies, waits for them, and re-layouts  2.87 us
    dot_general x2, matrix products, step(): jnp.dot(rows, cand_rows.T, preferred_element_type=jnp.float32)  2.86 us
  transfers between devices with their start and end apart: 1, of which 1 were waited for; matrix products, arithmetic and copies ran while one was open for 0% of the time, Pallas kernels for 0%

commit v1 on v0

--- a/solution.py
+++ b/solution.py
@@ -12,7 +12,10 @@
     my_index = lax.axis_index("item")
     my_local = lax.dynamic_slice_in_dim(cand_local, my_index * per_owner, per_owner)
     my_rows = item_table[my_local]
-    cand_rows = lax.all_gather(my_rows, "item", axis=0, tiled=True)
+    count_2 = lax.axis_size("item")
+    shards = jnp.stack([my_rows for _ in range(count_2)])
+    shards = lax.all_to_all(shards, "item", split_axis=0, concat_axis=0)
+    cand_rows = jnp.concatenate(shards, axis=0)
     slots = jnp.arange(total_cands, dtype=jnp.int32)
     tok_rows = hidden_states.shape[0]
     width = hidden_states.shape[1]

time: 88 us -> 86.5 us (0.983)
  blocking collectives: 30.1 us -> 19.3 us
  starting transfers between devices: 0.04 us -> 5.24 us
  waiting for transfers between devices: 34 us -> 36.7 us
  local copies, waits for them, and re-layouts: 3.5 us -> 4.82 us
    all_gather x1 -> x0, blocking collectives: 10.7 us -> none  [on_device(): cand_rows = lax.all_gather(my_rows, 'item', axis=0, tiled=True)]
    all_to_all x0 -> x1, starting transfers between devices: none -> 5.2 us  [on_device(): shards = lax.all_to_all(shards, 'item', split_axis=0, concat_axis=0)]
    all_to_all x0 -> x1, waiting for transfers between devices: none -> 3.64 us  [on_device(): shards = lax.all_to_all(shards, 'item', split_axis=0, concat_axis=0)]
    reduce_scatter x1, waiting for transfers between devices: 34 us -> 33.1 us  [on_device(): lax.psum_scatter(partial_grad, 'item', scatter_dimension=0, tiled=True)]
  transfers between devices with their start and end apart: 1 -> 2, of which waited for: 1 -> 2; matrix products, arithmetic and copies ran while one was open for 0% -> 0% of each run, Pallas kernels for 0% -> 0%
where the time goes in v1:
time: 86.5 us; the launch traced here: 86.2 us
  waiting for transfers between devices  36.7 us (42%)
  blocking collectives  19.3 us (22%)
  between operations  14.1 us (16%)
  matrix products  5.64 us (7%)
  starting transfers between devices  5.24 us (6%)
  local copies, waits for them, and re-layouts  4.82 us (6%)
    reduce_scatter x1, waiting for transfers between devices, on_device(): lax.psum_scatter(partial_grad, 'item', scatter_dimension=0, tiled=True)  33.1 us
    psum x1, blocking collectives, on_device(): owned = lax.psum(owned, 'dp')  19.3 us
    all_to_all x1, starting transfers between devices, on_device(): shards = lax.all_to_all(shards, 'item', split_axis=0, concat_axis=0)  5.2 us
    all_to_all x1, waiting for transfers between devices, on_device(): shards = lax.all_to_all(shards, 'item', split_axis=0, concat_axis=0)  3.64 us
    unnamed x14, local copies, waits for them, and re-layouts  3.55 us
    dot_general x2, matrix products, step(): jnp.dot(rows, cand_rows.T, preferred_element_type=jnp.float32)  2.85 us
  transfers between devices with their start and end apart: 2, of which 2 were waited for; matrix products, arithmetic and copies ran while one was open for 0% of the time, Pallas kernels for 0%

profile of v1, /device:TPU:0, one launch (start us, length us, event | category | flops | bytes accessed | tf_op | source)
XLA Modules:
  0.0 86.2 jit_solution(12820022731517037253)
XLA Ops:
  7.2 0.0 copy-start
  7.2 0.0 copy-start.6
  7.2 0.7 copy-done.6
  7.9 0.1 compare_select_fusion
  8.0 0.2 copy-done
  8.2 0.6 gather_fusion
  8.8 0.6 stack.2
  9.4 5.2 %all-to-all-start = ((bf16[8,8,512]{2,1,0:T(8,128)(2,1)}), bf16[8,8,512]{2,1,0:T(8,128)(2,1)S(1)}, u32[]{:S(2)}, u32[]{:S(2)}) async-start(bf16[8,8,512]{2,1,0:T(8,128)(2,1)} %stack.2), calls=%async_computation | async-start | bytes 131072 | tf_op jit(solution)/shard_map/all_to_all | solution.py:17
  14.6 0.0 copy-start.4
  14.6 0.0 reduce-scatter.2.cloned.1.call-start
  14.7 0.6 copy-done.4
  15.3 0.7 copy-done.5
  16.0 3.6 %all-to-all-done = bf16[8,8,512]{2,1,0:T(8,128)(2,1)S(1)} async-done(((bf16[8,8,512]{2,1,0:T(8,128)(2,1)}), bf16[8,8,512]{2,1,0:T(8,128)(2,1)S(1)}, u32[]{:S(2)}, u32[]{:S(2)}) %all-to-all-start) | async-done | bytes 65568 | tf_op jit(solution)/shard_map/all_to_all | solution.py:17
  19.7 0.7 copy-done.3
  20.3 4.2 %while.13 = (s32[]{:T(128)}, f32[64,512]{1,0:T(8,128)S(1)}, bf16[2,512,512]{2,1,0:T(8,128)(2,1)S(1)}, f32[2,512]{1,0:T(2,128)S(1)}, bf16[2,512,512]{2,1,0:T(8,12...) while((s32[]{:T(128)}, f32[64,512]{1,0:T(8,128)S(1)}, ...), condition=%wide.region_3.4_spmd.clone, body=%wide.region_0.3_spmd.clone.sunk | while | flops 101579776 | bytes 6716315 | solution.py:42
  20.3 1.4 %fusion.26 = (f32[512]{0:T(512)S(1)}, f32[512,64]{0,1:T(8,128)S(1)}) fusion(f32[64]{0:T(128)S(1)} %get-tuple-element.180, bf16[64,512]{1,0:T(8,128)(2,1)S(1)} %get-tuple-element.179, bf16[2,512,512]{2,1,0:T(8,128)(2,1)} %get-tuple-element.178, s32[]{:T(128)} %get-tuple-element.164), kind=kOutput, calls=%fused_computation.24.clone.1 | convolution fusion | flops 33619456 | bytes 723712 | tf_op jit(solution)/shard_map/while/body/eval_jaxpr/dot_general | solution.py:31
  21.8 0.3 fusion.28
  22.2 0.0 copy-done.1
  22.2 0.2 convolution_add_fusion.2
  22.4 0.0 copy-start.1
  22.4 1.4 %fusion.26 = (f32[512]{0:T(512)S(1)}, f32[512,64]{0,1:T(8,128)S(1)}) fusion(f32[64]{0:T(128)S(1)} %get-tuple-element.180, bf16[64,512]{1,0:T(8,128)(2,1)S(1)} %get-tuple-element.179, bf16[2,512,512]{2,1,0:T(8,128)(2,1)} %get-tuple-element.178, s32[]{:T(128)} %get-tuple-element.164), kind=kOutput, calls=%fused_computation.24.clone.1 | convolution fusion | flops 33619456 | bytes 723712 | tf_op jit(solution)/shard_map/while/body/eval_jaxpr/dot_general | solution.py:31
  23.9 0.3 fusion.28
  24.3 0.0 copy-done.1
  24.3 0.2 convolution_add_fusion.2
  24.6 0.0 copy-start.2
  24.6 0.0 copy-start.7
  24.6 0.6 copy-done.2
  25.2 0.0 reduce-scatter.2.cloned.1.call-update
  25.2 33.1 %reduce-scatter.2.cloned.1.call-done = f32[8,512]{1,0:T(8,128)} async-done(((f32[64,512]{1,0:T(8,128)}), f32[8,512]{1,0:T(8,128)}) %reduce-scatter.2.cloned.1.call-update) | async-done | bytes 16400 | tf_op jit(solution)/shard_map/reduce_scatter | solution.py:46
  58.3 19.3 %psum.7 = f32[8,512]{1,0:T(8,128)S(1)} all-reduce(f32[8,512]{1,0:T(8,128)} %reduce-scatter.2.cloned.1.call-done), channel_id=1, replica_groups=mesh['item'=8,'dp'=4] {'dp'}, use_global_device_ids=true, to_apply=%region_5.6 | all-reduce | flops 4096 | bytes 32768 | tf_op jit(solution)/shard_map/psum | solution.py:47
  77.6 1.7 %fusion.11 = f32[512,512]{1,0:T(8,128)} fusion(f32[8,512]{1,0:T(8,128)S(1)} %psum.7, s32[8]{0:T(128)S(1)} %get-tuple-element.98), kind=kOutput, calls=%fused_computation.20 | convolution fusion | flops 25169920 | bytes 1064992 | tf_op jit(solution)/shard_map/dot_general | solution.py:52
  79.3 0.0 copy-done.7
  (14 shorter events, 0.2 us)
Async XLA Ops:
  7.2 1.1 %copy-start = (bf16[512,512]{1,0:T(8,128)(2,1)S(1)}, bf16[512,512]{1,0:T(8,128)(2,1)}, u32[]{:S(2)}) copy-start(bf16[512,512]{1,0:T(8,128)(2,1)} %param.9) | copy-start | bytes 1572868
  7.2 0.7 copy-start.6
  9.4 10.2 %all-to-all-start = ((bf16[8,8,512]{2,1,0:T(8,128)(2,1)}), bf16[8,8,512]{2,1,0:T(8,128)(2,1)S(1)}, u32[]{:S(2)}, u32[]{:S(2)}) async-start(bf16[8,8,512]{2,1,0:T(8,128)(2,1)} %stack.2), calls=%async_computation | async-start | bytes 131072 | tf_op jit(solution)/shard_map/all_to_all | solution.py:17
  14.6 0.7 copy-start.4
  14.6 43.7 %reduce-scatter.2.cloned.1.call-start = ((), (), s32[]{:S(2)}) async-start(), calls=%async_computation.2 | async-start | bytes 147456 | tf_op jit(solution)/shard_map/reduce_scatter | solution.py:46
  15.3 0.7 copy-start.5
  19.7 0.7 copy-start.3
  20.3 1.9 %copy-start.1 = (bf16[2,512,512]{2,1,0:T(8,128)(2,1)S(1)}, bf16[2,512,512]{2,1,0:T(8,128)(2,1)}, u32[]{:S(2)}) copy-start(bf16[2,512,512]{2,1,0:T(8,128)(2,1)} %get-tuple-element.178) | copy-start | bytes 3145732 | tf_op jit(solution)/shard_map/while
  22.4 1.9 %copy-start.1 = (bf16[2,512,512]{2,1,0:T(8,128)(2,1)S(1)}, bf16[2,512,512]{2,1,0:T(8,128)(2,1)}, u32[]{:S(2)}) copy-start(bf16[2,512,512]{2,1,0:T(8,128)(2,1)} %get-tuple-element.178) | copy-start | bytes 3145732 | tf_op jit(solution)/shard_map/while
  24.6 0.7 copy-start.2
  24.6 54.7 %copy-start.7 = (bf16[2,512,512]{2,1,0:T(8,128)(2,1)}, bf16[2,512,512]{2,1,0:T(8,128)(2,1)S(1)}, u32[]{:S(2)}) copy-start(bf16[2,512,512]{2,1,0:T(8,128)(2,1)S(1)} %get-tuple-element.50) | copy-start | bytes 3145732
Sparse Core Ops, SparseCore 0:
  25.4 32.9 reduce-scatter.1
